TPU v7x, 32 devices: a whole 2x2x4 slice. The times are simulated.
32 devices in a mesh: ctx: 8 (over y, x, core), tp: 4 (over z).
Axes of the slice: x: 2, y: 2, z: 4, core: 2. Of those that a mesh axis runs over, the one named last changes fastest.
Arguments:
- queries: bfloat16 [4096, 32, 128], P('ctx', 'tp'), may hold values from -110 to 110
- keys: bfloat16 [4096, 32, 128], P('ctx', 'tp'), may hold values from -7 to 7
- values: bfloat16 [4096, 32, 128], P('ctx', 'tp'), may hold values from -6 to 6
- seg_lengths: int32 [256], replicated, may hold values from 1 to 32, 4096 in all
- out_weight: bfloat16 [4096, 4096], P('tp'), may hold values from -0.09375 to 0.09375
Outputs:
- mixed: bfloat16 [4096, 4096], P('ctx', 'tp')
Inputs may be any that keep to these rules, and one draw needn't show every extreme that they name: `seg_lengths`: the 256 segment lengths sum to 4096; the longest is exactly 32.
All inputs are finite; a program needn't handle non-finite values.
Results may differ from a plain program's by a relative error of at most 0.039.
Values may be sent and summed in bfloat16 or wider, within the bound.
A program may use at most 128 MiB of HBM per device.

v0:
```python
import functools

import jax
import jax.numpy as jnp
from jax import lax
from jax.experimental import pallas as pl
from jax.experimental.pallas import tpu as pltpu
from jax.sharding import PartitionSpec as P

ITERS = 6


very_negative = -1e30


def prefix(shard, axis, combine, identity):
    peers, index = (lax.axis_size(axis), lax.axis_index(axis))
    everything = jax.tree.map(
        lambda part, kind: lax.all_gather(part.astype(kind), axis),
        shard,
        (jnp.bfloat16, jnp.bfloat16, jnp.bfloat16),
    )
    start = jax.tree.map(
        lambda part, zero: jnp.broadcast_to(jnp.asarray(zero, part.dtype), part.shape),
        shard,
        identity,
    )

    def lap(k, before):
        reached = k < index
        new = combine(
            before, jax.tree.map(lambda part, own: part[k].astype(own.dtype), everything, shard)
        )
        return jax.tree.map(lambda a, b: jnp.where(reached, a, b), new, before)

    return lax.fori_loop(0, peers, lap, start)


def merge_states(earlier, latter):
    top_peak = jnp.maximum(earlier[0], latter[0])
    first_factor = jnp.exp(earlier[0] - top_peak)
    second_factor = jnp.exp(latter[0] - top_peak)
    return (
        top_peak,
        earlier[1] * first_factor + latter[1] * second_factor,
        earlier[2] * first_factor[..., None] + latter[2] * second_factor[..., None],
    )


def masked_weights(scores, allowed):
    masked = jnp.where(allowed, scores, very_negative)
    top_score = jnp.max(masked, axis=-1, keepdims=True)
    expo = jnp.where(allowed, jnp.exp(masked - top_score), 0.0)
    return expo / jnp.maximum(jnp.sum(expo, axis=-1, keepdims=True), 1.0)


def newton_inverse(attention_kernel):
    highest = lax.Precision.HIGHEST
    row_sum = jnp.max(jnp.sum(attention_kernel, axis=2), axis=-1)
    col_sum = jnp.max(jnp.sum(attention_kernel, axis=1), axis=-1)
    approx = jnp.swapaxes(attention_kernel, 1, 2) / (row_sum * col_sum)[:, None, None]
    identity = jnp.eye(attention_kernel.shape[-1], dtype=jnp.float32)
    for iteration in range(ITERS):
        applied = jnp.einsum("hij,hjk->hik", attention_kernel, approx, precision=highest)
        factor = 7.0 * identity - applied
        factor = 15.0 * identity - jnp.einsum("hij,hjk->hik", applied, factor, precision=highest)
        factor = 13.0 * identity - jnp.einsum("hij,hjk->hik", applied, factor, precision=highest)
        approx = 0.25 * jnp.einsum("hij,hjk->hik", approx, factor, precision=highest)
    return approx


def on_device(queries, keys, values, seg_lengths, out_weight):
    row_count, heads_here, head_dim = queries.shape
    landmarks = seg_lengths.shape[0]
    score_scale_factor = head_dim ** (-0.5)
    block_start = lax.axis_index("ctx") * row_count
    seg_ends = jnp.cumsum(seg_lengths)
    seg_begins = seg_ends - seg_lengths
    position = block_start + jnp.arange(row_count, dtype=jnp.int32)
    block_member_mask = (
        (position[None, :] >= seg_begins[:, None]) & (position[None, :] < seg_ends[:, None])
    ).astype(jnp.bfloat16)
    query_block_sums = jnp.einsum(
        "na,abf->bnf", block_member_mask, queries, preferred_element_type=jnp.float32
    )
    key_block_sums = jnp.einsum(
        "na,abf->bnf", block_member_mask, keys, preferred_element_type=jnp.float32
    )
    query_block_sums, key_block_sums = (
        lax.psum(query_block_sums.astype(jnp.bfloat16), "ctx").astype(jnp.float32),
        lax.psum(key_block_sums.astype(jnp.bfloat16), "ctx").astype(jnp.float32),
    )
    seg_root = jnp.sqrt(seg_lengths.astype(jnp.float32))[None, :, None]
    landmark_query_rows = (query_block_sums / seg_root).astype(jnp.bfloat16)
    landmark_key_rows = (key_block_sums / seg_root).astype(jnp.bfloat16)
    state_score_matrix = (
        jnp.einsum("fcb,pfb->fcp", landmark_query_rows, keys, preferred_element_type=jnp.float32)
        * score_scale_factor
    )
    state_peak = jnp.max(state_score_matrix, axis=-1)
    state_exponent = jnp.exp(state_score_matrix - state_peak[..., None])
    state_total = jnp.sum(state_exponent, axis=-1)
    state_running_total = jnp.einsum(
        "ogq,qoc->ogc",
        state_exponent.astype(jnp.bfloat16),
        values,
        preferred_element_type=jnp.float32,
    )
    start_state = (
        jnp.full((heads_here, landmarks), very_negative, jnp.float32),
        jnp.zeros((heads_here, landmarks), jnp.float32),
        jnp.zeros((heads_here, landmarks, head_dim), jnp.float32),
    )
    in_peak, in_total, in_acc = prefix(
        (state_peak, state_total, state_running_total), "ctx", merge_states, start_state
    )
    attention_kernel = jax.nn.softmax(
        jnp.einsum(
            "slu,szu->slz",
            landmark_query_rows,
            landmark_key_rows,
            preferred_element_type=jnp.float32,
        )
        * score_scale_factor,
        axis=-1,
    )
    pseudo_inverse_matrix = newton_inverse(attention_kernel)
    causal = jnp.arange(row_count)[:, None] >= jnp.arange(row_count)[None, :]
    local_scores = (
        jnp.einsum("thd,uhd->htu", queries, keys, preferred_element_type=jnp.float32)
        * score_scale_factor
    )
    local_scores = jnp.where(causal[None], local_scores, very_negative)
    local_probs = jax.nn.softmax(local_scores, axis=-1).astype(jnp.bfloat16)
    local_block_output = jnp.einsum(
        "htu,uhd->thd", local_probs, values, preferred_element_type=jnp.float32
    )
    allowed = seg_ends <= block_start
    landmark_value_rows = jnp.where(
        allowed[None, :, None], in_acc / jnp.maximum(in_total, 1.0)[..., None], 0.0
    )
    blended_state = jnp.einsum(
        "bxz,bzl->bxl", pseudo_inverse_matrix, landmark_value_rows, precision=lax.Precision.HIGHEST
    ).astype(jnp.bfloat16)
    landmark_score_matrix = (
        jnp.einsum("byz,yfz->ybf", queries, landmark_key_rows, preferred_element_type=jnp.float32)
        * score_scale_factor
    )
    landmark_weight_matrix = masked_weights(landmark_score_matrix, allowed[None, None, :]).astype(
        jnp.bfloat16
    )
    land_out = jnp.einsum(
        "ecp,epy->cey", landmark_weight_matrix, blended_state, preferred_element_type=jnp.float32
    )
    landmark_attention_layer = (
        (local_block_output + land_out)
        .astype(jnp.bfloat16)
        .reshape(row_count, heads_here * head_dim)
    )
    partial_value = jnp.dot(
        landmark_attention_layer, out_weight, preferred_element_type=jnp.float32
    )
    return lax.psum_scatter(
        partial_value.astype(jnp.bfloat16), "tp", scatter_dimension=1, tiled=True
    )


MESH_ID = pl.DeviceIdType.MESH
HIGHEST = lax.Precision.HIGHEST
NT = (((1,), (1,)), ((), ()))
TN = (((0,), (0,)), ((), ()))


def front_kernel(
    n, q_ref, k_ref, v_ref, len_row_ref, len_col_ref, out_ref,
    sum_out, sum_in, land, acc_out, acc_in, stat_out, stat_in,
    mix_out, mix_in, local, weights, send_sem, recv_sem,
):
    heads, rows, hd = q_ref.shape
    marks = len_row_ref.shape[1]
    scale = hd ** (-0.5)
    me = lax.axis_index("ctx")
    f32, bf16 = jnp.float32, jnp.bfloat16

    def push(phase, src, dst, peer):
        return pltpu.make_async_remote_copy(
            src_ref=src, dst_ref=dst,
            send_sem=send_sem.at[phase, peer], recv_sem=recv_sem.at[phase, me],
            device_id={"ctx": peer}, device_id_type=MESH_ID,
        )

    def arrival(phase, src, dst, peer):
        return pltpu.make_async_remote_copy(
            src_ref=src, dst_ref=dst,
            send_sem=send_sem.at[phase, peer], recv_sem=recv_sem.at[phase, peer],
            device_id={"ctx": peer}, device_id_type=MESH_ID,
        )

    barrier = pltpu.get_barrier_semaphore()
    for o in range(1, n):
        pl.semaphore_signal(
            barrier, inc=1, device_id={"ctx": lax.rem(me + o, n)}, device_id_type=MESH_ID
        )

    low = lax.broadcasted_iota(jnp.int32, (marks, marks), 0)
    high = lax.broadcasted_iota(jnp.int32, (marks, marks), 1)
    len_row = len_row_ref[...].astype(f32)
    len_col = len_col_ref[...].astype(f32)
    ends_col = jnp.sum(jnp.where(high <= low, len_row, 0.0), axis=1, keepdims=True)
    ends_row = jnp.sum(jnp.where(low <= high, len_col, 0.0), axis=0, keepdims=True)
    begins_col = ends_col - len_col
    root_col = jnp.sqrt(len_col)
    position = (
        me * rows + lax.broadcasted_iota(jnp.int32, (marks, rows), 1)
    ).astype(f32)
    member = jnp.where(
        (position >= begins_col) & (position < ends_col), 1.0, 0.0
    ).astype(bf16)

    def block_sums(p):
        return (
            jnp.dot(member, q_ref[p], preferred_element_type=f32).astype(bf16),
            jnp.dot(member, k_ref[p], preferred_element_type=f32).astype(bf16),
        )

    pl.semaphore_wait(barrier, n - 1)

    def send_sums(o, _):
        p = lax.rem(me + o, n)
        sum_out[p, 0], sum_out[p, 1] = block_sums(p)
        push(0, sum_out.at[p], sum_in.at[me], p).start()
        return 0

    lax.fori_loop(1, n, send_sums, 0)
    own_q, own_k = block_sums(me)
    sum_in[me, 0] = own_q
    sum_in[me, 1] = own_k

    half = rows // 2
    low_t = lax.broadcasted_iota(jnp.int32, (half, half), 0)
    low_u = lax.broadcasted_iota(jnp.int32, (half, half), 1)
    diagonal = low_t >= low_u

    def local_head(h, _):
        q, k, v = q_ref[h], k_ref[h], v_ref[h]
        s0 = lax.dot_general(q[:half], k[:half], NT, preferred_element_type=f32) * scale
        s0 = jnp.where(diagonal, s0, very_negative)
        e0 = jnp.exp(s0 - jnp.max(s0, axis=1, keepdims=True))
        n0 = jnp.sum(e0, axis=1, keepdims=True)
        local[h, :half] = jnp.dot(e0.astype(bf16), v[:half], preferred_element_type=f32) / n0
        s1 = lax.dot_general(q[half:], k[:half], NT, preferred_element_type=f32) * scale
        s2 = lax.dot_general(q[half:], k[half:], NT, preferred_element_type=f32) * scale
        s2 = jnp.where(diagonal, s2, very_negative)
        top = jnp.maximum(
            jnp.max(s1, axis=1, keepdims=True), jnp.max(s2, axis=1, keepdims=True)
        )
        e1 = jnp.exp(s1 - top)
        e2 = jnp.exp(s2 - top)
        n1 = jnp.sum(e1, axis=1, keepdims=True) + jnp.sum(e2, axis=1, keepdims=True)
        local[h, half:] = (
            jnp.dot(e1.astype(bf16), v[:half], preferred_element_type=f32)
            + jnp.dot(e2.astype(bf16), v[half:], preferred_element_type=f32)
        ) / n1
        return 0

    lax.fori_loop(0, heads, local_head, 0)

    def wait_sums(o, total):
        p = lax.rem(me + o, n)
        arrival(0, sum_out.at[p], sum_in.at[p], p).wait_recv()
        return (total[0] + sum_in[p, 0].astype(f32), total[1] + sum_in[p, 1].astype(f32))

    q_sum, k_sum = lax.fori_loop(
        1, n, wait_sums, (sum_in[me, 0].astype(f32), sum_in[me, 1].astype(f32))
    )
    land_q = (q_sum / root_col).astype(bf16)
    land_k = (k_sum / root_col).astype(bf16)
    land[me, 0] = land_q
    land[me, 1] = land_k

    def send_land(o, _):
        p = lax.rem(me + o, n)
        push(1, land.at[me], land.at[me], p).start()
        return 0

    lax.fori_loop(1, n, send_land, 0)

    def highest(a, b):
        return jnp.dot(a, b, precision=HIGHEST, preferred_element_type=f32)

    scores = lax.dot_general(land_q, land_k, NT, preferred_element_type=f32) * scale
    expo = jnp.exp(scores - jnp.max(scores, axis=1, keepdims=True))
    kernel = expo / jnp.sum(expo, axis=1, keepdims=True)
    row_sum = jnp.max(jnp.sum(kernel, axis=1, keepdims=True), axis=0, keepdims=True)
    col_sum = jnp.max(jnp.sum(kernel, axis=0, keepdims=True), axis=1, keepdims=True)
    eye = jnp.where(low == high, 1.0, 0.0).astype(f32)

    def newton(_, z):
        kz = highest(kernel, z)
        f = 15.0 * eye - highest(kz, 7.0 * eye - kz)
        f = 13.0 * eye - highest(kz, f)
        return 0.25 * highest(z, f)

    pinv = lax.fori_loop(0, ITERS, newton, kernel.T / (row_sum * col_sum))

    def block_state(p):
        st = lax.dot_general(k_ref[p], land[p, 0], NT, preferred_element_type=f32) * scale
        peak = jnp.max(st, axis=0, keepdims=True)
        e = jnp.exp(st - peak)
        total = jnp.sum(e, axis=0, keepdims=True)
        acc = lax.dot_general(v_ref[p], e.astype(bf16), TN, preferred_element_type=f32)
        line = lax.broadcasted_iota(jnp.int32, (8, marks), 0)
        return acc.astype(bf16), jnp.where(line == 0, peak, total)

    def send_states(o, _):
        p = lax.rem(me + o, n)
        arrival(1, land.at[p], land.at[p], p).wait_recv()
        acc_out[p], stat_out[p] = block_state(p)
        push(2, acc_out.at[p], acc_in.at[me], p).start()
        push(3, stat_out.at[p], stat_in.at[me], p).start()
        return 0

    lax.fori_loop(1, n, send_states, 0)
    own_acc, own_stat = block_state(me)
    acc_in[me] = own_acc
    stat_in[me] = own_stat

    allowed_here = ends_row <= (me * rows).astype(f32)

    def land_head(h, _):
        s = lax.dot_general(q_ref[h], land[h, 1], NT, preferred_element_type=f32) * scale
        s = jnp.where(allowed_here, s, very_negative)
        e = jnp.where(allowed_here, jnp.exp(s - jnp.max(s, axis=1, keepdims=True)), 0.0)
        weights[h] = (e / jnp.maximum(jnp.sum(e, axis=1, keepdims=True), 1.0)).astype(bf16)
        return 0

    lax.fori_loop(0, heads, land_head, 0)

    def scan_block(b, carry):
        peak, total, acc = carry
        allowed = ends_row <= (b * rows).astype(f32)
        lv = jnp.where(allowed, acc / jnp.maximum(total, 1.0), 0.0)
        mixed = lax.dot_general(
            lv, pinv, NT, precision=HIGHEST, preferred_element_type=f32
        ).astype(bf16)

        @pl.when(b == me)
        def _():
            mix_in[me] = mixed

        @pl.when(b != me)
        def _():
            mix_out[b] = mixed
            push(4, mix_out.at[b], mix_in.at[me], b).start()
            arrival(2, acc_out.at[b], acc_in.at[b], b).wait_recv()
            arrival(3, stat_out.at[b], stat_in.at[b], b).wait_recv()

        stat = stat_in[b]
        new_peak, new_total = stat[0:1], stat[1:2]
        top = jnp.maximum(peak, new_peak)
        first = jnp.exp(peak - top)
        second = jnp.exp(new_peak - top)
        return (
            top,
            total * first + new_total * second,
            acc * first + acc_in[b].astype(f32) * second,
        )

    lax.fori_loop(
        0, n, scan_block,
        (
            jnp.full((1, marks), very_negative, f32),
            jnp.zeros((1, marks), f32),
            jnp.zeros((hd, marks), f32),
        ),
    )

    def finish(o, _):
        h = lax.rem(me + o, n)

        @pl.when(h != me)
        def _():
            arrival(4, mix_out.at[h], mix_in.at[h], h).wait_recv()

        land_out = lax.dot_general(weights[h], mix_in[h], NT, preferred_element_type=f32)
        at = pl.multiple_of(h * hd, hd)
        out_ref[:, pl.ds(at, hd)] = (local[h] + land_out).astype(bf16)
        return 0

    lax.fori_loop(0, n, finish, 0)

    def drain(o, _):
        p = lax.rem(me + o, n)
        push(0, sum_out.at[p], sum_in.at[me], p).wait_send()
        push(1, land.at[me], land.at[me], p).wait_send()
        push(2, acc_out.at[p], acc_in.at[me], p).wait_send()
        push(3, stat_out.at[p], stat_in.at[me], p).wait_send()
        push(4, mix_out.at[p], mix_in.at[me], p).wait_send()
        return 0

    lax.fori_loop(1, n, drain, 0)


def front(queries, keys, values, seg_lengths):
    rows, heads, hd = queries.shape
    n = lax.axis_size("ctx")
    marks = seg_lengths.shape[0]
    by_head = lambda x: jnp.swapaxes(x, 0, 1)
    bf16, f32 = jnp.bfloat16, jnp.float32
    return pl.pallas_call(
        functools.partial(front_kernel, n),
        out_shape=jax.ShapeDtypeStruct((rows, heads * hd), bf16),
        in_specs=[pl.BlockSpec(memory_space=pltpu.VMEM)] * 5,
        out_specs=pl.BlockSpec(memory_space=pltpu.VMEM),
        scratch_shapes=[
            pltpu.VMEM((n, 2, marks, hd), bf16),
            pltpu.VMEM((n, 2, marks, hd), bf16),
            pltpu.VMEM((n, 2, marks, hd), bf16),
            pltpu.VMEM((n, hd, marks), bf16),
            pltpu.VMEM((n, hd, marks), bf16),
            pltpu.VMEM((n, 8, marks), f32),
            pltpu.VMEM((n, 8, marks), f32),
            pltpu.VMEM((n, hd, marks), bf16),
            pltpu.VMEM((n, hd, marks), bf16),
            pltpu.VMEM((heads, rows, hd), f32),
            pltpu.VMEM((heads, rows, marks), bf16),
            pltpu.SemaphoreType.DMA((5, n)),
            pltpu.SemaphoreType.DMA((5, n)),
        ],
        compiler_params=pltpu.CompilerParams(
            collective_id=0, has_side_effects=True, vmem_limit_bytes=40 << 20
        ),
        name="front",
    )(
        by_head(queries), by_head(keys), by_head(values),
        seg_lengths[None, :], seg_lengths[:, None],
    )


def on_device_by_head(queries, keys, values, seg_lengths, out_weight):
    attention = front(queries, keys, values, seg_lengths)
    partial_value = jnp.dot(attention, out_weight, preferred_element_type=jnp.float32)
    return lax.psum_scatter(
        partial_value.astype(jnp.bfloat16), "tp", scatter_dimension=1, tiled=True
    )


def on_device_any(queries, keys, values, seg_lengths, out_weight):
    one_head_each = queries.shape[1] == lax.axis_size("ctx")
    body = on_device_by_head if one_head_each else on_device
    return body(queries, keys, values, seg_lengths, out_weight)


def solution(mesh):
    in_specs = (
        P("ctx", "tp", None),
        P("ctx", "tp", None),
        P("ctx", "tp", None),
        P(),
        P("tp", None),
    )
    out_specs = P("ctx", "tp")
    return jax.shard_map(
        on_device_any, mesh=mesh, in_specs=in_specs, out_specs=out_specs, check_vma=False
    )
```

profile of v0, /device:TPU:15, one launch (start us, length us, event | category | flops | bytes accessed | tf_op | source)
XLA Modules:
  0.0 152.8 jit_solution(432477409673438412)
XLA Ops:
  6.5 0.0 reduce-scatter.2.cloned.1.call-start
  6.5 0.8 copy.12.len_col_ref
  7.3 1.4 copy.16
  8.7 1.9 %copy_bitcast_fusion = (bf16[8,512,128]{2,1,0:T(8,128)(2,1)S(1)}, bf16[8,512,128]{2,1,0:T(8,128)(2,1)S(1)}) fusion(bf16[512,8,128]{2,1,0:T(8,128)(2,1)} %param.7, bf16[512,8,128]{2,1,0:T(8,128)(2,1)} %param.6), kind=kLoop, calls=%fused_computation.1 | loop fusion | bytes 4194304 | tf_op jit(solution)/shard_map/transpose | solution.py:408
  10.7 0.0 copy-start
  10.7 0.7 copy-done
  11.3 47.6 %front.1 = bf16[512,1024]{1,0:T(8,128)(2,1)S(1)} custom-call(bf16[8,512,128]{2,1,0:T(8,128)(2,1)S(1)} %bitcast.11, bf16[8,512,128]{2,1,0:T(8,128)(2,1)S(1)} %get-tuple-element.6.k_ref, bf16[8,512,128]{2,1,0:T(8,128)(2,1)S(1)} %get-tuple-element.5.v_ref, s32[1,256]{1,0:T(1,128)S(1)} %bitcast.13, s32[256,1]{1,0:T(8,128)S(1)} %copy.12.len_col_ref), custom_call_target="tpu_custom_call" | custom-call | tf_op jit(solution)/shard_map/front/pallas_call | solution.py:410
  59.0 9.4 %convolution_convert_fusion = bf16[512,4096]{1,0:T(8,128)(2,1)} fusion(bf16[512,1024]{1,0:T(8,128)(2,1)S(1)} %front.1, bf16[1024,4096]{1,0:T(8,128)(2,1)} %param.9), kind=kOutput, calls=%fused_computation | convolution fusion | flops 4297064448 | bytes 13631488 | tf_op jit(solution)/shard_map/dot_general | solution.py:442
  68.4 0.0 reduce-scatter.2.cloned.1.call-update
  68.4 77.5 %reduce-scatter.2.cloned.1.call-done = bf16[512,1024]{1,0:T(8,128)(2,1)} async-done(((bf16[512,4096]{1,0:T(8,128)(2,1)}), bf16[512,1024]{1,0:T(8,128)(2,1)}) %reduce-scatter.2.cloned.1.call-update) | async-done | bytes 1048592 | tf_op jit(solution)/shard_map/reduce_scatter | solution.py:443
Async XLA Ops:
  6.5 139.4 %reduce-scatter.2.cloned.1.call-start = ((), (), s32[]{:S(2)}) async-start(), calls=%async_computation.1 | async-start | bytes 5242880 | tf_op jit(solution)/shard_map/reduce_scatter | solution.py:443
  10.7 0.7 copy-start
Sparse Core Ops, SparseCore 0:
  68.6 77.3 reduce-scatter.1
where the time goes:
time: 155 us; the launch traced here: 153 us
  waiting for transfers between devices  77.6 us (50%)
  Pallas kernels  47.6 us (31%)
  between operations  13.4 us (9%)
  matrix products  9.43 us (6%)
  local copies, waits for them, and re-layouts  4.77 us (3%)
    reduce_scatter x1, waiting for transfers between devices, on_device_by_head(): lax.psum_scatter(partial_value.astype(jnp.bfloat16), 'tp', scatter_dimens...  77.5 us
    pallas_call x1, Pallas kernels, front(): pl.pallas_call(functools.partial(front_kernel, n), out_shape=jax.ShapeDty...  47.6 us
    dot_general x1, matrix products, on_device_by_head(): jnp.dot(attention, out_weight, preferred_element_type=jnp.float32)  9.43 us
  transfers between devices with their start and end apart: 1, of which 1 were waited for; matrix products, arithmetic and copies ran while one was open for 0% of the time, Pallas kernels for 0%

commit v1 on v0

--- a/solution.py
+++ b/solution.py
@@ -167,14 +167,17 @@
 
 MESH_ID = pl.DeviceIdType.MESH
 HIGHEST = lax.Precision.HIGHEST
+CHUNKS = 4
 NT = (((1,), (1,)), ((), ()))
 TN = (((0,), (0,)), ((), ()))
 
 
-def front_kernel(
-    n, q_ref, k_ref, v_ref, len_row_ref, len_col_ref, out_ref,
+def layer_kernel(
+    n, q_ref, k_ref, v_ref, len_row_ref, len_col_ref, w_hbm, out_ref,
     sum_out, sum_in, land, acc_out, acc_in, stat_out, stat_in,
-    mix_out, mix_in, local, weights, send_sem, recv_sem,
+    mix_out, mix_in, local, weights, att, w_own, w_outer,
+    far_out, near_out, cross_out, own_out, outer_in, att_in, far_in, cross_in,
+    send_sem, recv_sem, load_sem, wsend_sem, wrecv_sem, zsend_sem, zrecv_sem,
 ):
     heads, rows, hd = q_ref.shape
     marks = len_row_ref.shape[1]
@@ -196,7 +199,78 @@
             device_id={"ctx": peer}, device_id_type=MESH_ID,
         )
 
+    t = lax.axis_index("tp")
+    side = t // 2
+    near_end, far_end = 3 * side, 3 - 3 * side
+    mid, cross = 1 + side, 2 - side
+    is_end = (t == near_end)
+    is_mid = (t == mid)
+    cols = out_ref.shape[1]
+    chunk = rows // CHUNKS
+
+    loads = [
+        pltpu.make_async_copy(
+            w_hbm.at[:, pl.ds(j * cols, cols)], w_own.at[j], load_sem.at[j]
+        )
+        for j in range(4)
+    ]
+    for load in loads:
+        load.start()
+
+    core = lax.rem(me, 2)
+    sibling = me + 1 - 2 * core
+    part = w_hbm.shape[0] // 2
+    part_rows = pl.ds(pl.multiple_of(core * part, part), part)
+    other_rows = pl.ds(pl.multiple_of(part - core * part, part), part)
+
+    def weight_hop(i, column):
+        return pltpu.make_async_remote_copy(
+            src_ref=w_hbm.at[part_rows, pl.ds(pl.multiple_of(column * cols, cols), cols)],
+            dst_ref=w_outer.at[i, part_rows],
+            send_sem=wsend_sem.at[i], recv_sem=wrecv_sem.at[i],
+            device_id={"tp": mid}, device_id_type=MESH_ID,
+        )
+
+    def weight_share(i, which):
+        return pltpu.make_async_remote_copy(
+            src_ref=w_outer.at[i, which], dst_ref=w_outer.at[i, which],
+            send_sem=wsend_sem.at[2 + i], recv_sem=wrecv_sem.at[2 + i],
+            device_id={"ctx": sibling}, device_id_type=MESH_ID,
+        )
+
+    def line_copy(kind, c, src, dst, to):
+        at = pl.ds(c * chunk, chunk)
+        return pltpu.make_async_remote_copy(
+            src_ref=src.at[at], dst_ref=dst.at[at],
+            send_sem=zsend_sem.at[kind, c], recv_sem=zrecv_sem.at[kind, c],
+            device_id={"tp": to}, device_id_type=MESH_ID,
+        )
+
+    def project(dst, first, count, src, w, j, add=None):
+        step = 256
+        here = pl.ds(first, count)
+
+        def tile(i, _):
+            at = pl.ds(pl.multiple_of(i * step, step), step)
+            y = jnp.dot(src[here], w[j, :, at], preferred_element_type=f32)
+            if add is not None:
+                y = y + add[here, at].astype(f32)
+            dst[here, at] = y.astype(bf16)
+            return 0
+
+        lax.fori_loop(0, cols // step, tile, 0)
+
     barrier = pltpu.get_barrier_semaphore()
+
+    @pl.when(is_end)
+    def _():
+        pl.semaphore_signal(barrier, inc=1, device_id={"tp": mid}, device_id_type=MESH_ID)
+
+    @pl.when(is_mid)
+    def _():
+        pl.semaphore_signal(barrier, inc=1, device_id={"tp": near_end}, device_id_type=MESH_ID)
+        pl.semaphore_signal(barrier, inc=1, device_id={"tp": cross}, device_id_type=MESH_ID)
+
     for o in range(1, n):
         pl.semaphore_signal(
             barrier, inc=1, device_id={"ctx": lax.rem(me + o, n)}, device_id_type=MESH_ID
@@ -223,7 +297,18 @@
             jnp.dot(member, k_ref[p], preferred_element_type=f32).astype(bf16),
         )
 
-    pl.semaphore_wait(barrier, n - 1)
+    @pl.when(is_end)
+    def _():
+        pl.semaphore_wait(barrier, n)
+
+    @pl.when(is_mid)
+    def _():
+        pl.semaphore_wait(barrier, n + 1)
+
+    @pl.when(is_end)
+    def _():
+        weight_hop(0, mid).start()
+        weight_hop(1, cross).start()
 
     def send_sums(o, _):
         p = lax.rem(me + o, n)
@@ -384,10 +469,78 @@
 
         land_out = lax.dot_general(weights[h], mix_in[h], NT, preferred_element_type=f32)
         at = pl.multiple_of(h * hd, hd)
-        out_ref[:, pl.ds(at, hd)] = (local[h] + land_out).astype(bf16)
+        att[:, pl.ds(at, hd)] = (local[h] + land_out).astype(bf16)
         return 0
 
     lax.fori_loop(0, n, finish, 0)
+    for load in loads:
+        load.wait()
+
+    @pl.when(is_end)
+    def _():
+        for c in range(CHUNKS):
+            project(far_out, c * chunk, chunk, att, w_own, far_end)
+            if c >= 2:
+                line_copy(0, c - 2, far_out, outer_in, mid).wait_send()
+            line_copy(0, c, far_out, outer_in, mid).start()
+        project(own_out, 0, rows, att, w_own, t)
+        for c in range(CHUNKS):
+            if c < 2:
+                line_copy(0, CHUNKS - 2 + c, far_out, outer_in, mid).wait_send()
+            else:
+                line_copy(1, c - 2, att, att_in, mid).wait_send()
+            line_copy(1, c, att, att_in, mid).start()
+        for c in range(CHUNKS):
+            at = pl.ds(c * chunk, chunk)
+            line_copy(4, c, near_out, outer_in, mid).wait_recv()
+            out_ref[at] = (own_out[at].astype(f32) + outer_in[at].astype(f32)).astype(bf16)
+        for c in range(CHUNKS - 2, CHUNKS):
+            line_copy(1, c, att, att_in, mid).wait_send()
+        weight_hop(0, mid).wait_send()
+        weight_hop(1, cross).wait_send()
+
+    @pl.when(is_mid)
+    def _():
+        project(far_out, 0, rows, att, w_own, far_end)
+        for i in range(2):
+            weight_hop(i, mid).wait_recv()
+            weight_share(i, part_rows).start()
+        project(near_out, 0, rows, att, w_own, near_end)
+        project(cross_out, 0, rows, att, w_own, cross)
+        project(own_out, 0, rows, att, w_own, t)
+
+        def pass_near(c):
+            at = pl.ds(c * chunk, chunk)
+            line_copy(2, c, far_out, far_in, cross).wait_recv()
+            near_out[at] = (near_out[at].astype(f32) + far_in[at].astype(f32)).astype(bf16)
+            line_copy(4, c, near_out, outer_in, near_end).start()
+
+        for c in range(CHUNKS):
+            at = pl.ds(c * chunk, chunk)
+            line_copy(0, c, far_out, outer_in, near_end).wait_recv()
+            far_out[at] = (far_out[at].astype(f32) + outer_in[at].astype(f32)).astype(bf16)
+            line_copy(2, c, far_out, far_in, cross).start()
+            if c >= 1:
+                pass_near(c - 1)
+        for i in range(2):
+            weight_share(i, other_rows).wait_recv()
+        for c in range(CHUNKS):
+            line_copy(1, c, att, att_in, near_end).wait_recv()
+            project(cross_out, c * chunk, chunk, att_in, w_outer, 1, cross_out)
+            line_copy(3, c, cross_out, cross_in, cross).start()
+            project(own_out, c * chunk, chunk, att_in, w_outer, 0, own_out)
+            if c == 0:
+                pass_near(CHUNKS - 1)
+        for c in range(CHUNKS):
+            at = pl.ds(c * chunk, chunk)
+            line_copy(3, c, cross_out, cross_in, cross).wait_recv()
+            out_ref[at] = (own_out[at].astype(f32) + cross_in[at].astype(f32)).astype(bf16)
+        for i in range(2):
+            weight_share(i, part_rows).wait_send()
+        for c in range(CHUNKS):
+            line_copy(2, c, far_out, far_in, cross).wait_send()
+            line_copy(3, c, cross_out, cross_in, cross).wait_send()
+            line_copy(4, c, near_out, outer_in, near_end).wait_send()
 
     def drain(o, _):
         p = lax.rem(me + o, n)
@@ -401,16 +554,19 @@
     lax.fori_loop(1, n, drain, 0)
 
 
-def front(queries, keys, values, seg_lengths):
+def layer(queries, keys, values, seg_lengths, out_weight):
     rows, heads, hd = queries.shape
     n = lax.axis_size("ctx")
     marks = seg_lengths.shape[0]
+    depth = out_weight.shape[0]
+    cols = out_weight.shape[1] // 4
     by_head = lambda x: jnp.swapaxes(x, 0, 1)
     bf16, f32 = jnp.bfloat16, jnp.float32
     return pl.pallas_call(
-        functools.partial(front_kernel, n),
-        out_shape=jax.ShapeDtypeStruct((rows, heads * hd), bf16),
-        in_specs=[pl.BlockSpec(memory_space=pltpu.VMEM)] * 5,
+        functools.partial(layer_kernel, n),
+        out_shape=jax.ShapeDtypeStruct((rows, cols), bf16),
+        in_specs=[pl.BlockSpec(memory_space=pltpu.VMEM)] * 5
+        + [pl.BlockSpec(memory_space=pl.ANY)],
         out_specs=pl.BlockSpec(memory_space=pltpu.VMEM),
         scratch_shapes=[
             pltpu.VMEM((n, 2, marks, hd), bf16),
@@ -424,30 +580,38 @@
             pltpu.VMEM((n, hd, marks), bf16),
             pltpu.VMEM((heads, rows, hd), f32),
             pltpu.VMEM((heads, rows, marks), bf16),
+            pltpu.VMEM((rows, depth), bf16),
+            pltpu.VMEM((4, depth, cols), bf16),
+            pltpu.VMEM((2, depth, cols), bf16),
+            pltpu.VMEM((rows, cols), bf16),
+            pltpu.VMEM((rows, cols), bf16),
+            pltpu.VMEM((rows, cols), bf16),
+            pltpu.VMEM((rows, cols), bf16),
+            pltpu.VMEM((rows, cols), bf16),
+            pltpu.VMEM((rows, depth), bf16),
+            pltpu.VMEM((rows, cols), bf16),
+            pltpu.VMEM((rows, cols), bf16),
             pltpu.SemaphoreType.DMA((5, n)),
             pltpu.SemaphoreType.DMA((5, n)),
+            pltpu.SemaphoreType.DMA((4,)),
+            pltpu.SemaphoreType.DMA((4,)),
+            pltpu.SemaphoreType.DMA((4,)),
+            pltpu.SemaphoreType.DMA((5, CHUNKS)),
+            pltpu.SemaphoreType.DMA((5, CHUNKS)),
         ],
         compiler_params=pltpu.CompilerParams(
-            collective_id=0, has_side_effects=True, vmem_limit_bytes=40 << 20
+            collective_id=0, has_side_effects=True, vmem_limit_bytes=56 << 20
         ),
-        name="front",
+        name="layer",
     )(
         by_head(queries), by_head(keys), by_head(values),
-        seg_lengths[None, :], seg_lengths[:, None],
-    )
-
-
-def on_device_by_head(queries, keys, values, seg_lengths, out_weight):
-    attention = front(queries, keys, values, seg_lengths)
-    partial_value = jnp.dot(attention, out_weight, preferred_element_type=jnp.float32)
-    return lax.psum_scatter(
-        partial_value.astype(jnp.bfloat16), "tp", scatter_dimension=1, tiled=True
+        seg_lengths[None, :], seg_lengths[:, None], out_weight,
     )
 
 
 def on_device_any(queries, keys, values, seg_lengths, out_weight):
     one_head_each = queries.shape[1] == lax.axis_size("ctx")
-    body = on_device_by_head if one_head_each else on_device
+    body = layer if one_head_each and lax.axis_size("tp") == 4 else on_device
     return body(queries, keys, values, seg_lengths, out_weight)
 
 

time: 155 us -> 118 us (0.76); the launches traced: 153 us -> 118 us
  waiting for transfers between devices: 77.6 us -> 0 us
  Pallas kernels: 47.6 us -> 109 us
  between operations: 13.4 us -> 0.01 us
  matrix products: 9.43 us -> 0 us
  local copies, waits for them, and re-layouts: 4.77 us -> 9.32 us
    reduce_scatter x1 -> x0, waiting for transfers between devices: 77.5 us -> none  [on_device_by_head(): lax.psum_scatter(partial_value.astype(jnp.bfloat16), 'tp', scatter_dimens...]
    pallas_call x1, Pallas kernels: 47.6 us -> 109 us  [layer(): pl.pallas_call(functools.partial(layer_kernel, n), out_shape=jax.ShapeDty...]
    dot_general x1 -> x0, matrix products: 9.43 us -> none  [on_device_by_head(): jnp.dot(attention, out_weight, preferred_element_type=jnp.float32)]
    unnamed x3 -> x2, local copies, waits for them, and re-layouts: 2.04 us -> 4.59 us
  transfers between devices with their start and end apart: 1 -> 0, of which waited for: 1 -> 0; matrix products, arithmetic and copies ran while one was open for 0% -> 0% of each run, Pallas kernels for 0% -> 0%
where the time goes in v1:
time: 118 us
  Pallas kernels  109 us (92%)
  local copies, waits for them, and re-layouts  9.32 us (8%)
    pallas_call x1, Pallas kernels, layer(): pl.pallas_call(functools.partial(layer_kernel, n), out_shape=jax.ShapeDty...  109 us
    unnamed x2, local copies, waits for them, and re-layouts  4.59 us
    transpose x1, local copies, waits for them, and re-layouts, layer(): by_head = lambda x: jnp.swapaxes(x, 0, 1)  3.26 us

profile of v1, /device:TPU:15, one launch (start us, length us, event | category | flops | bytes accessed | tf_op | source)
XLA Modules:
  0.0 117.8 jit_solution(18093599460407248731)
XLA Ops:
  0.0 1.5 %copy.12.len_col_ref = s32[256,1]{1,0:T(8,128)} copy(s32[256,1]{0,1:T(1,128)} %bitcast.10) | data formatting | bytes 2048 | tf_op jit(solution)/shard_map/broadcast_in_dim | solution.py:608
  1.5 2.3 %copy.16 = bf16[512,8,128]{2,0,1:T(8,128)(2,1)} copy(bf16[512,8,128]{2,1,0:T(8,128)(2,1)} %param.5) | data formatting | bytes 2097152 | tf_op args[0]
  3.8 3.3 %copy_bitcast_fusion = (bf16[8,512,128]{2,1,0:T(8,128)(2,1)}, bf16[8,512,128]{2,1,0:T(8,128)(2,1)}) fusion(bf16[512,8,128]{2,1,0:T(8,128)(2,1)} %param.7, bf16[512,8,128]{2,1,0:T(8,128)(2,1)} %param.6), kind=kLoop, calls=%fused_computation | loop fusion | bytes 4194304 | tf_op jit(solution)/shard_map/transpose | solution.py:563
  7.1 108.5 %layer.1 = bf16[512,1024]{1,0:T(8,128)(2,1)} custom-call(bf16[8,512,128]{2,1,0:T(8,128)(2,1)} %bitcast.9, bf16[8,512,128]{2,1,0:T(8,128)(2,1)} %get-tuple-element.6.k_ref, bf16[8,512,128]{2,1,0:T(8,128)(2,1)} %get-tuple-element.5.v_ref, s32[1,256]{1,0:T(1,128)} %bitcast.11, s32[256,1]{1,0:T(8,128)} %copy.12.len_col_ref, bf16[1024,4096]{1,0:T(8,128)(2,1)} %w_hbm.1), custom_call_target="tpu_custom_call" | custom-call | tf_op jit(solution)/shard_map/layer/pallas_call | solution.py:565
  115.6 2.3 %copy.18 = bf16[512,1024]{1,0:T(8,128)(2,1)} copy(bf16[512,1024]{1,0:T(8,128)(2,1)} %layer.1) | data formatting | bytes 2097152

commit v2 on v1

--- a/solution.py
+++ b/solution.py
@@ -167,20 +167,21 @@
 
 MESH_ID = pl.DeviceIdType.MESH
 HIGHEST = lax.Precision.HIGHEST
-CHUNKS = 4
+CHUNKS = 8
+DEPTH = 3
 NT = (((1,), (1,)), ((), ()))
 TN = (((0,), (0,)), ((), ()))
 
 
 def layer_kernel(
-    n, q_ref, k_ref, v_ref, len_row_ref, len_col_ref, w_hbm, out_ref,
+    n, q_ref, k_ref, v_ref, len_ref, w_hbm, out_ref,
     sum_out, sum_in, land, acc_out, acc_in, stat_out, stat_in,
     mix_out, mix_in, local, weights, att, w_own, w_outer,
     far_out, near_out, cross_out, own_out, outer_in, att_in, far_in, cross_in,
     send_sem, recv_sem, load_sem, wsend_sem, wrecv_sem, zsend_sem, zrecv_sem,
 ):
     heads, rows, hd = q_ref.shape
-    marks = len_row_ref.shape[1]
+    marks = len_ref.shape[1]
     scale = hd ** (-0.5)
     me = lax.axis_index("ctx")
     f32, bf16 = jnp.float32, jnp.bfloat16
@@ -219,23 +220,29 @@
 
     core = lax.rem(me, 2)
     sibling = me + 1 - 2 * core
-    part = w_hbm.shape[0] // 2
-    part_rows = pl.ds(pl.multiple_of(core * part, part), part)
-    other_rows = pl.ds(pl.multiple_of(part - core * part, part), part)
+    part = w_hbm.shape[0] // 4
+    axis_bit = (2, 4)
+
+    def flipped(i, p):
+        return p + axis_bit[i] - 2 * axis_bit[i] * lax.rem(p // axis_bit[i], 2)
+
+    def quarter(i, p):
+        q = 2 * lax.rem(p // axis_bit[i], 2) + lax.rem(p, 2)
+        return pl.ds(pl.multiple_of(q * part, part), part)
 
     def weight_hop(i, column):
         return pltpu.make_async_remote_copy(
-            src_ref=w_hbm.at[part_rows, pl.ds(pl.multiple_of(column * cols, cols), cols)],
-            dst_ref=w_outer.at[i, part_rows],
+            src_ref=w_hbm.at[quarter(i, me), pl.ds(pl.multiple_of(column * cols, cols), cols)],
+            dst_ref=w_outer.at[i, quarter(i, me)],
             send_sem=wsend_sem.at[i], recv_sem=wrecv_sem.at[i],
             device_id={"tp": mid}, device_id_type=MESH_ID,
         )
 
-    def weight_share(i, which):
+    def weight_share(i, step, owner, to):
         return pltpu.make_async_remote_copy(
-            src_ref=w_outer.at[i, which], dst_ref=w_outer.at[i, which],
-            send_sem=wsend_sem.at[2 + i], recv_sem=wrecv_sem.at[2 + i],
-            device_id={"ctx": sibling}, device_id_type=MESH_ID,
+            src_ref=w_outer.at[i, quarter(i, owner)], dst_ref=w_outer.at[i, quarter(i, owner)],
+            send_sem=wsend_sem.at[2 * step + i], recv_sem=wrecv_sem.at[2 * step + i],
+            device_id={"ctx": to}, device_id_type=MESH_ID,
         )
 
     def line_copy(kind, c, src, dst, to):
@@ -278,8 +285,8 @@
 
     low = lax.broadcasted_iota(jnp.int32, (marks, marks), 0)
     high = lax.broadcasted_iota(jnp.int32, (marks, marks), 1)
-    len_row = len_row_ref[...].astype(f32)
-    len_col = len_col_ref[...].astype(f32)
+    len_row = len_ref[...].astype(f32)
+    len_col = jnp.broadcast_to(len_row, (8, marks)).T[:, 0:1]
     ends_col = jnp.sum(jnp.where(high <= low, len_row, 0.0), axis=1, keepdims=True)
     ends_row = jnp.sum(jnp.where(low <= high, len_col, 0.0), axis=0, keepdims=True)
     begins_col = ends_col - len_col
@@ -310,16 +317,44 @@
         weight_hop(0, mid).start()
         weight_hop(1, cross).start()
 
-    def send_sums(o, _):
-        p = lax.rem(me + o, n)
+    def twin(p):
+        return p + 1 - 2 * lax.rem(p, 2)
+
+    def hand(phase, src, dst, sent, landed):
+        return pltpu.make_async_remote_copy(
+            src_ref=src, dst_ref=dst,
+            send_sem=send_sem.at[phase, sent], recv_sem=recv_sem.at[phase, landed],
+            device_id={"ctx": sibling}, device_id_type=MESH_ID,
+        )
+
+    def send_twin(i, _):
+        p = twin(lax.rem(me + 2 * i, n))
         sum_out[p, 0], sum_out[p, 1] = block_sums(p)
-        push(0, sum_out.at[p], sum_in.at[me], p).start()
-        return 0
-
-    lax.fori_loop(1, n, send_sums, 0)
-    own_q, own_k = block_sums(me)
-    sum_in[me, 0] = own_q
-    sum_in[me, 1] = own_k
+        hand(0, sum_out.at[p], sum_in.at[p], p, p).start()
+        return 0
+
+    def chip_sums(p):
+        q_part, k_part = block_sums(p)
+        hand(0, sum_out.at[p], sum_in.at[p], p, p).wait_recv()
+        return (
+            (q_part.astype(f32) + sum_in[p, 0].astype(f32)),
+            (k_part.astype(f32) + sum_in[p, 1].astype(f32)),
+        )
+
+    def send_sums(i, _):
+        p = lax.rem(me + 2 * i, n)
+        q_part, k_part = chip_sums(p)
+        sum_out[p, 0] = q_part.astype(bf16)
+        sum_out[p, 1] = k_part.astype(bf16)
+        push(5, sum_out.at[p], sum_in.at[sibling], p).start()
+        return 0
+
+    lax.fori_loop(1, n // 2, send_twin, 0)
+    send_twin(0, 0)
+    lax.fori_loop(1, n // 2, send_sums, 0)
+    own_q, own_k = chip_sums(me)
+    sum_out[me, 0] = own_q.astype(bf16)
+    sum_out[me, 1] = own_k.astype(bf16)
 
     half = rows // 2
     low_t = lax.broadcasted_iota(jnp.int32, (half, half), 0)
@@ -350,25 +385,35 @@
 
     lax.fori_loop(0, heads, local_head, 0)
 
-    def wait_sums(o, total):
-        p = lax.rem(me + o, n)
-        arrival(0, sum_out.at[p], sum_in.at[p], p).wait_recv()
-        return (total[0] + sum_in[p, 0].astype(f32), total[1] + sum_in[p, 1].astype(f32))
+    def wait_sums(i, total):
+        p = lax.rem(me + 2 * i, n)
+        slot = twin(p)
+        arrival(5, sum_out.at[p], sum_in.at[slot], p).wait_recv()
+        return (total[0] + sum_in[slot, 0].astype(f32), total[1] + sum_in[slot, 1].astype(f32))
 
     q_sum, k_sum = lax.fori_loop(
-        1, n, wait_sums, (sum_in[me, 0].astype(f32), sum_in[me, 1].astype(f32))
+        1, n // 2, wait_sums, (sum_out[me, 0].astype(f32), sum_out[me, 1].astype(f32))
     )
     land_q = (q_sum / root_col).astype(bf16)
     land_k = (k_sum / root_col).astype(bf16)
-    land[me, 0] = land_q
-    land[me, 1] = land_k
-
-    def send_land(o, _):
-        p = lax.rem(me + o, n)
-        push(1, land.at[me], land.at[me], p).start()
-        return 0
-
-    lax.fori_loop(1, n, send_land, 0)
+    land[0, me] = land_q
+    land[1, me] = land_k
+
+    LAND = (1, 6)
+
+    def land_push(kind, p):
+        return push(LAND[kind], land.at[kind, me], land.at[kind, me], p)
+
+    def land_hand(kind, p):
+        return hand(LAND[kind], land.at[kind, p], land.at[kind, p], twin(p), p)
+
+    for kind in range(2):
+        for i in range(1, n // 2):
+            land_push(kind, lax.rem(me + 2 * i, n)).start()
+        land_hand(kind, me).start()
+
+    def land_wait(kind, p):
+        arrival(LAND[kind], land.at[kind, p], land.at[kind, p], p).wait_recv()
 
     def highest(a, b):
         return jnp.dot(a, b, precision=HIGHEST, preferred_element_type=f32)
@@ -386,10 +431,8 @@
         f = 13.0 * eye - highest(kz, f)
         return 0.25 * highest(z, f)
 
-    pinv = lax.fori_loop(0, ITERS, newton, kernel.T / (row_sum * col_sum))
-
     def block_state(p):
-        st = lax.dot_general(k_ref[p], land[p, 0], NT, preferred_element_type=f32) * scale
+        st = lax.dot_general(k_ref[p], land[0, p], NT, preferred_element_type=f32) * scale
         peak = jnp.max(st, axis=0, keepdims=True)
         e = jnp.exp(st - peak)
         total = jnp.sum(e, axis=0, keepdims=True)
@@ -397,23 +440,60 @@
         line = lax.broadcasted_iota(jnp.int32, (8, marks), 0)
         return acc.astype(bf16), jnp.where(line == 0, peak, total)
 
-    def send_states(o, _):
-        p = lax.rem(me + o, n)
-        arrival(1, land.at[p], land.at[p], p).wait_recv()
+    def send_state(p):
         acc_out[p], stat_out[p] = block_state(p)
         push(2, acc_out.at[p], acc_in.at[me], p).start()
         push(3, stat_out.at[p], stat_in.at[me], p).start()
-        return 0
-
-    lax.fori_loop(1, n, send_states, 0)
+
     own_acc, own_stat = block_state(me)
     acc_in[me] = own_acc
     stat_in[me] = own_stat
+    early = lax.fori_loop(0, 2, newton, kernel.T / (row_sum * col_sum))
+
+    def relay_q(i, _):
+        p = lax.rem(me + 2 * i, n)
+        land_wait(0, p)
+        land_hand(0, p).start()
+        return 0
+
+    lax.fori_loop(1, n // 2, relay_q, 0)
+
+    def near_states(i, _):
+        send_state(lax.rem(me + 2 * i, n))
+        return 0
+
+    lax.fori_loop(1, n // 2, near_states, 0)
+
+    def relay_k(i, _):
+        p = lax.rem(me + 2 * i, n)
+        land_wait(1, p)
+        land_hand(1, p).start()
+        return 0
+
+    lax.fori_loop(1, n // 2, relay_k, 0)
+
+    early = lax.fori_loop(2, 3, newton, early)
+
+    def twin_states(i, _):
+        p = twin(lax.rem(me + 2 * i, n))
+        land_wait(0, p)
+        send_state(p)
+        return 0
+
+    lax.fori_loop(1, n // 2, twin_states, 0)
+    twin_states(0, 0)
+    pinv = lax.fori_loop(3, ITERS, newton, early)
+
+    def wait_k(i, _):
+        land_wait(1, twin(lax.rem(me + 2 * i, n)))
+        return 0
+
+    lax.fori_loop(0, n // 2, wait_k, 0)
 
     allowed_here = ends_row <= (me * rows).astype(f32)
 
     def land_head(h, _):
-        s = lax.dot_general(q_ref[h], land[h, 1], NT, preferred_element_type=f32) * scale
+        s = lax.dot_general(q_ref[h], land[1, h], NT, preferred_element_type=f32) * scale
         s = jnp.where(allowed_here, s, very_negative)
         e = jnp.where(allowed_here, jnp.exp(s - jnp.max(s, axis=1, keepdims=True)), 0.0)
         weights[h] = (e / jnp.maximum(jnp.sum(e, axis=1, keepdims=True), 1.0)).astype(bf16)
@@ -480,21 +560,21 @@
     def _():
         for c in range(CHUNKS):
             project(far_out, c * chunk, chunk, att, w_own, far_end)
-            if c >= 2:
-                line_copy(0, c - 2, far_out, outer_in, mid).wait_send()
+            if c >= DEPTH:
+                line_copy(0, c - DEPTH, far_out, outer_in, mid).wait_send()
             line_copy(0, c, far_out, outer_in, mid).start()
         project(own_out, 0, rows, att, w_own, t)
         for c in range(CHUNKS):
-            if c < 2:
-                line_copy(0, CHUNKS - 2 + c, far_out, outer_in, mid).wait_send()
+            if c < DEPTH:
+                line_copy(0, CHUNKS - DEPTH + c, far_out, outer_in, mid).wait_send()
             else:
-                line_copy(1, c - 2, att, att_in, mid).wait_send()
+                line_copy(1, c - DEPTH, att, att_in, mid).wait_send()
             line_copy(1, c, att, att_in, mid).start()
         for c in range(CHUNKS):
             at = pl.ds(c * chunk, chunk)
             line_copy(4, c, near_out, outer_in, mid).wait_recv()
             out_ref[at] = (own_out[at].astype(f32) + outer_in[at].astype(f32)).astype(bf16)
-        for c in range(CHUNKS - 2, CHUNKS):
+        for c in range(CHUNKS - DEPTH, CHUNKS):
             line_copy(1, c, att, att_in, mid).wait_send()
         weight_hop(0, mid).wait_send()
         weight_hop(1, cross).wait_send()
@@ -504,10 +584,8 @@
         project(far_out, 0, rows, att, w_own, far_end)
         for i in range(2):
             weight_hop(i, mid).wait_recv()
-            weight_share(i, part_rows).start()
-        project(near_out, 0, rows, att, w_own, near_end)
-        project(cross_out, 0, rows, att, w_own, cross)
-        project(own_out, 0, rows, att, w_own, t)
+            weight_share(i, 1, me, flipped(i, me)).start()
+            weight_share(i, 2, me, sibling).start()
 
         def pass_near(c):
             at = pl.ds(c * chunk, chunk)
@@ -520,10 +598,21 @@
             line_copy(0, c, far_out, outer_in, near_end).wait_recv()
             far_out[at] = (far_out[at].astype(f32) + outer_in[at].astype(f32)).astype(bf16)
             line_copy(2, c, far_out, far_in, cross).start()
+            if c == 0:
+                project(near_out, 0, rows, att, w_own, near_end)
+            if c == 1:
+                project(cross_out, 0, rows, att, w_own, cross)
+            if c == 2:
+                project(own_out, 0, rows, att, w_own, t)
             if c >= 1:
                 pass_near(c - 1)
+            if c == CHUNKS // 2:
+                for i in range(2):
+                    weight_share(i, 1, flipped(i, me), flipped(i, me)).wait_recv()
+                    weight_share(i, 3, flipped(i, me), sibling).start()
         for i in range(2):
-            weight_share(i, other_rows).wait_recv()
+            weight_share(i, 2, sibling, sibling).wait_recv()
+            weight_share(i, 3, flipped(i, sibling), sibling).wait_recv()
         for c in range(CHUNKS):
             line_copy(1, c, att, att_in, near_end).wait_recv()
             project(cross_out, c * chunk, chunk, att_in, w_outer, 1, cross_out)
@@ -536,7 +625,9 @@
             line_copy(3, c, cross_out, cross_in, cross).wait_recv()
             out_ref[at] = (own_out[at].astype(f32) + cross_in[at].astype(f32)).astype(bf16)
         for i in range(2):
-            weight_share(i, part_rows).wait_send()
+            weight_share(i, 1, me, flipped(i, me)).wait_send()
+            weight_share(i, 2, me, sibling).wait_send()
+            weight_share(i, 3, flipped(i, me), sibling).wait_send()
         for c in range(CHUNKS):
             line_copy(2, c, far_out, far_in, cross).wait_send()
             line_copy(3, c, cross_out, cross_in, cross).wait_send()
@@ -544,14 +635,30 @@
 
     def drain(o, _):
         p = lax.rem(me + o, n)
-        push(0, sum_out.at[p], sum_in.at[me], p).wait_send()
-        push(1, land.at[me], land.at[me], p).wait_send()
         push(2, acc_out.at[p], acc_in.at[me], p).wait_send()
         push(3, stat_out.at[p], stat_in.at[me], p).wait_send()
         push(4, mix_out.at[p], mix_in.at[me], p).wait_send()
         return 0
 
     lax.fori_loop(1, n, drain, 0)
+
+    def drain_pairs(i, _):
+        p = lax.rem(me + 2 * i, n)
+        push(5, sum_out.at[p], sum_in.at[sibling], p).wait_send()
+        for kind in range(2):
+            land_push(kind, p).wait_send()
+        return 0
+
+    lax.fori_loop(1, n // 2, drain_pairs, 0)
+
+    def drain_hands(i, _):
+        p = lax.rem(me + 2 * i, n)
+        hand(0, sum_out.at[twin(p)], sum_in.at[twin(p)], twin(p), twin(p)).wait_send()
+        for kind in range(2):
+            land_hand(kind, p).wait_send()
+        return 0
+
+    lax.fori_loop(0, n // 2, drain_hands, 0)
 
 
 def layer(queries, keys, values, seg_lengths, out_weight):
@@ -565,13 +672,13 @@
     return pl.pallas_call(
         functools.partial(layer_kernel, n),
         out_shape=jax.ShapeDtypeStruct((rows, cols), bf16),
-        in_specs=[pl.BlockSpec(memory_space=pltpu.VMEM)] * 5
+        in_specs=[pl.BlockSpec(memory_space=pltpu.VMEM)] * 4
         + [pl.BlockSpec(memory_space=pl.ANY)],
         out_specs=pl.BlockSpec(memory_space=pltpu.VMEM),
         scratch_shapes=[
             pltpu.VMEM((n, 2, marks, hd), bf16),
             pltpu.VMEM((n, 2, marks, hd), bf16),
-            pltpu.VMEM((n, 2, marks, hd), bf16),
+            pltpu.VMEM((2, n, marks, hd), bf16),
             pltpu.VMEM((n, hd, marks), bf16),
             pltpu.VMEM((n, hd, marks), bf16),
             pltpu.VMEM((n, 8, marks), f32),
@@ -591,11 +698,11 @@
             pltpu.VMEM((rows, depth), bf16),
             pltpu.VMEM((rows, cols), bf16),
             pltpu.VMEM((rows, cols), bf16),
-            pltpu.SemaphoreType.DMA((5, n)),
-            pltpu.SemaphoreType.DMA((5, n)),
+            pltpu.SemaphoreType.DMA((7, n)),
+            pltpu.SemaphoreType.DMA((7, n)),
             pltpu.SemaphoreType.DMA((4,)),
-            pltpu.SemaphoreType.DMA((4,)),
-            pltpu.SemaphoreType.DMA((4,)),
+            pltpu.SemaphoreType.DMA((8,)),
+            pltpu.SemaphoreType.DMA((8,)),
             pltpu.SemaphoreType.DMA((5, CHUNKS)),
             pltpu.SemaphoreType.DMA((5, CHUNKS)),
         ],
@@ -605,7 +712,7 @@
         name="layer",
     )(
         by_head(queries), by_head(keys), by_head(values),
-        seg_lengths[None, :], seg_lengths[:, None], out_weight,
+        seg_lengths[None, :], out_weight,
     )
 
 

time: 118 us -> 111 us (0.941)
  Pallas kernels: 109 us -> 103 us
  local copies, waits for them, and re-layouts: 9.32 us -> 7.85 us
    pallas_call x1, Pallas kernels: 109 us -> 103 us  [layer(): pl.pallas_call(functools.partial(layer_kernel, n), out_shape=jax.ShapeDty...]
    broadcast_in_dim x1 -> x0, local copies, waits for them, and re-layouts: 1.47 us -> none  [layer(): seg_lengths[:, None]]
where the time goes in v2:
time: 111 us
  Pallas kernels  103 us (93%)
  local copies, waits for them, and re-layouts  7.85 us (7%)
    pallas_call x1, Pallas kernels, layer(): pl.pallas_call(functools.partial(layer_kernel, n), out_shape=jax.ShapeDty...  103 us
    unnamed x2, local copies, waits for them, and re-layouts  4.59 us
    transpose x1, local copies, waits for them, and re-layouts, layer(): by_head = lambda x: jnp.swapaxes(x, 0, 1)  3.26 us

profile of v2, /device:TPU:15, one launch (start us, length us, event | category | flops | bytes accessed | tf_op | source)
XLA Modules:
  0.0 111.0 jit_solution(13439333768525308060)
XLA Ops:
  0.0 2.3 %copy.12 = bf16[512,8,128]{2,0,1:T(8,128)(2,1)} copy(bf16[512,8,128]{2,1,0:T(8,128)(2,1)} %param.5) | data formatting | bytes 2097152 | tf_op args[0]
  2.3 3.3 %copy_bitcast_fusion = (bf16[8,512,128]{2,1,0:T(8,128)(2,1)}, bf16[8,512,128]{2,1,0:T(8,128)(2,1)}) fusion(bf16[512,8,128]{2,1,0:T(8,128)(2,1)} %param.7, bf16[512,8,128]{2,1,0:T(8,128)(2,1)} %param.6), kind=kLoop, calls=%fused_computation | loop fusion | bytes 4194304 | tf_op jit(solution)/shard_map/transpose | solution.py:670
  5.6 103.1 %layer.1 = bf16[512,1024]{1,0:T(8,128)(2,1)} custom-call(bf16[8,512,128]{2,1,0:T(8,128)(2,1)} %bitcast.8, bf16[8,512,128]{2,1,0:T(8,128)(2,1)} %get-tuple-element.6.k_ref, bf16[8,512,128]{2,1,0:T(8,128)(2,1)} %get-tuple-element.5.v_ref, s32[1,256]{1,0:T(1,128)} %bitcast.9, bf16[1024,4096]{1,0:T(8,128)(2,1)} %w_hbm.1), custom_call_target="tpu_custom_call" | custom-call | tf_op jit(solution)/shard_map/layer/pallas_call | solution.py:672
  108.7 2.3 %copy.14 = bf16[512,1024]{1,0:T(8,128)(2,1)} copy(bf16[512,1024]{1,0:T(8,128)(2,1)} %layer.1) | data formatting | bytes 2097152

commit v3 on v2

--- a/solution.py
+++ b/solution.py
@@ -415,8 +415,16 @@
     def land_wait(kind, p):
         arrival(LAND[kind], land.at[kind, p], land.at[kind, p], p).wait_recv()
 
-    def highest(a, b):
-        return jnp.dot(a, b, precision=HIGHEST, preferred_element_type=f32)
+    def split(a):
+        top = a.astype(bf16)
+        return top, (a - top.astype(f32)).astype(bf16)
+
+    def product(a, b):
+        return (
+            jnp.dot(a[0], b[1], preferred_element_type=f32)
+            + jnp.dot(a[1], b[0], preferred_element_type=f32)
+            + jnp.dot(a[0], b[0], preferred_element_type=f32)
+        )
 
     scores = lax.dot_general(land_q, land_k, NT, preferred_element_type=f32) * scale
     expo = jnp.exp(scores - jnp.max(scores, axis=1, keepdims=True))
@@ -425,11 +433,15 @@
     col_sum = jnp.max(jnp.sum(kernel, axis=0, keepdims=True), axis=1, keepdims=True)
     eye = jnp.where(low == high, 1.0, 0.0).astype(f32)
 
+    kernel_parts = split(kernel)
+
     def newton(_, z):
-        kz = highest(kernel, z)
-        f = 15.0 * eye - highest(kz, 7.0 * eye - kz)
-        f = 13.0 * eye - highest(kz, f)
-        return 0.25 * highest(z, f)
+        z_parts = split(z)
+        kz = product(kernel_parts, z_parts)
+        kz_parts = split(kz)
+        f = 15.0 * eye - product(kz_parts, split(7.0 * eye - kz))
+        f = 13.0 * eye - product(kz_parts, split(f))
+        return 0.25 * product(z_parts, split(f))
 
     def block_state(p):
         st = lax.dot_general(k_ref[p], land[0, p], NT, preferred_element_type=f32) * scale

time: 111 us -> 108 us (0.973)
  Pallas kernels: 103 us -> 99.5 us
    pallas_call x1, Pallas kernels: 103 us -> 99.5 us  [layer(): pl.pallas_call(functools.partial(layer_kernel, n), out_shape=jax.ShapeDty...]
where the time goes in v3:
time: 108 us; the launch traced here: 107 us
  Pallas kernels  99.5 us (92%)
  local copies, waits for them, and re-layouts  7.85 us (7%)
    pallas_call x1, Pallas kernels, layer(): pl.pallas_call(functools.partial(layer_kernel, n), out_shape=jax.ShapeDty...  99.5 us
    unnamed x2, local copies, waits for them, and re-layouts  4.59 us
    transpose x1, local copies, waits for them, and re-layouts, layer(): by_head = lambda x: jnp.swapaxes(x, 0, 1)  3.26 us

profile of v3, /device:TPU:15, one launch (start us, length us, event | category | flops | bytes accessed | tf_op | source)
XLA Modules:
  0.0 107.3 jit_solution(8386858785716588677)
XLA Ops:
  0.0 2.3 %copy.12 = bf16[512,8,128]{2,0,1:T(8,128)(2,1)} copy(bf16[512,8,128]{2,1,0:T(8,128)(2,1)} %param.5) | data formatting | bytes 2097152 | tf_op args[0]
  2.3 3.3 %copy_bitcast_fusion = (bf16[8,512,128]{2,1,0:T(8,128)(2,1)}, bf16[8,512,128]{2,1,0:T(8,128)(2,1)}) fusion(bf16[512,8,128]{2,1,0:T(8,128)(2,1)} %param.7, bf16[512,8,128]{2,1,0:T(8,128)(2,1)} %param.6), kind=kLoop, calls=%fused_computation | loop fusion | bytes 4194304 | tf_op jit(solution)/shard_map/transpose | solution.py:682
  5.6 99.5 %layer.1 = bf16[512,1024]{1,0:T(8,128)(2,1)} custom-call(bf16[8,512,128]{2,1,0:T(8,128)(2,1)} %bitcast.8, bf16[8,512,128]{2,1,0:T(8,128)(2,1)} %get-tuple-element.6.k_ref, bf16[8,512,128]{2,1,0:T(8,128)(2,1)} %get-tuple-element.5.v_ref, s32[1,256]{1,0:T(1,128)} %bitcast.9, bf16[1024,4096]{1,0:T(8,128)(2,1)} %w_hbm.1), custom_call_target="tpu_custom_call" | custom-call | tf_op jit(solution)/shard_map/layer/pallas_call | solution.py:684
  105.1 2.3 %copy.14 = bf16[512,1024]{1,0:T(8,128)(2,1)} copy(bf16[512,1024]{1,0:T(8,128)(2,1)} %layer.1) | data formatting | bytes 2097152
